TPU v7x, 256 devices: a whole 4x4x8 slice. The times are simulated.
256 devices in a mesh: beam: 8 (over x, core), row: 32 (over y, z).
Axes of the slice: x: 4, y: 4, z: 8, core: 2. Of those that a mesh axis runs over, the one named last changes fastest.
Arguments:
- x_in: bfloat16 [4, 2, 16, 8192], P(None, None, None, 'beam'), may hold values from -6 to 6
- w_inner: bfloat16 [8192, 2, 16384], P('beam', None, 'row'), may hold values from -0.0625 to 0.0625
- w_bc: bfloat16 [8192, 2, 2048], P('beam', None, 'row'), may hold values from -0.0625 to 0.0625
- w_dt: bfloat16 [8192, 256], P('beam', 'row'), may hold values from -0.0625 to 0.0625
- conv_x_w: bfloat16 [4, 16384], P(None, 'row'), may hold values from -3 to 3
- conv_bc_w: bfloat16 [4, 2, 2048], P(None, None, 'row'), may hold values from -3 to 3
- dt_bias: float32 [256], P('row'), may hold values from -4 to 1
- a_log: float32 [256], P('row'), may hold values from 0 to 2.8
- d_skip: float32 [256], P('row'), may hold values from 0.5 to 2
- norm_gain: float32 [16384], P('row'), may hold values from 0.1 to 1.9
- w_out: bfloat16 [16384, 8192], P('row', 'beam'), may hold values from -0.046875 to 0.046875
- ssm_state: bfloat16 [2, 16, 256, 64, 256], P(None, 'beam', 'row'), may hold values from -6 to 6
- conv_x_state: bfloat16 [2, 16, 256, 64, 3], P(None, 'beam', 'row'), may hold values from -6 to 6
- conv_bc_state: bfloat16 [2, 16, 3, 2, 2048], P(None, 'beam', None, None, 'row'), may hold values from -6 to 6
- parents: int32 [4, 2, 16], replicated, may hold values from 0 to 15
Outputs:
- layer_out: bfloat16 [4, 32, 8192], P(None, 'row', 'beam')
- ssm_final: bfloat16 [2, 16, 256, 64, 256], P(None, 'beam', 'row')
- conv_x_final: bfloat16 [2, 16, 256, 64, 3], P(None, 'beam', 'row')
- conv_bc_final: bfloat16 [2, 16, 3, 2, 2048], P(None, 'beam', None, None, 'row')
All inputs are finite; a program needn't handle non-finite values.
Results may differ from a plain program's by a relative error of at most 0.0077.
Values may be sent and summed in bfloat16 or wider, within the bound.
No kernel may reach another device: no remote copies, remote signals or barrier semaphores. Data moves between devices by JAX's collectives and lax.ppermute only.
A program may use at most 64 MiB of HBM per device.

v0:
```python
import jax
import jax.numpy as jnp
from jax import lax
from jax.sharding import PartitionSpec as P

HEADS = 256
HDIM = 64
GROUPS = 8
EPS = 1e-05


def partner_2(shard, axis, stride):
    return lax.ppermute(shard, axis, [(i, i ^ 1 << stride) for i in range(lax.axis_size(axis))])


def stored(value):
    return lax.optimization_barrier(value.astype(jnp.bfloat16))


def local(
    x_in,
    w_inner,
    w_bc,
    w_dt,
    conv_x_w,
    conv_bc_w,
    dt_bias,
    a_log,
    d_skip,
    norm_gain,
    w_out,
    ssm_state,
    conv_x_state,
    conv_bc_state,
    parents,
):
    beam_index = lax.axis_index("beam")
    row_index = lax.axis_index("row")
    steps_all, sessions, width, d_local = x_in.shape
    local_beams = ssm_state.shape[1]
    heads_local = ssm_state.shape[2]
    head_dim = ssm_state.shape[3]
    tap_count = conv_x_w.shape[0]
    group_heads = HEADS // GROUPS
    group_index = row_index * heads_local // group_heads
    group_span = lax.axis_size("row") // GROUPS
    swap_rounds = group_span.bit_length() - 1
    w_inner4 = w_inner.reshape(d_local, 2, heads_local, head_dim)
    w_out3 = w_out.reshape(heads_local, head_dim, w_out.shape[1])
    conv_taps = conv_x_w.astype(jnp.float32).reshape(tap_count, heads_local, head_dim)
    gains = norm_gain.reshape(heads_local, head_dim)
    bc_taps = conv_bc_w.astype(jnp.float32)
    decay_rates = jnp.exp(a_log)
    group_mask = (jnp.arange(GROUPS, dtype=jnp.int32) == group_index).astype(jnp.float32)
    ssm_held = ssm_state
    conv_held = conv_x_state
    rim_held = conv_bc_state
    outputs = []
    for step in range(steps_all):
        parent = parents[step]
        own_parent = lax.dynamic_slice_in_dim(parent, beam_index * local_beams, local_beams, 1)
        pieces = (
            lax.all_gather(ssm_held, "beam", axis=1, tiled=True),
            lax.all_gather(conv_held, "beam", axis=1, tiled=True),
            lax.all_gather(rim_held, "beam", axis=1, tiled=True),
        )
        span_size = pieces[0].shape[1]
        beam_ids = jnp.arange(span_size, dtype=jnp.int32)
        choose = (own_parent[:, :, None] == beam_ids[None, None, :]).astype(jnp.bfloat16)
        ssm_held = jnp.einsum(
            "sij,sjhpn->sihpn", choose, pieces[0], preferred_element_type=jnp.float32
        ).astype(jnp.bfloat16)
        conv_held = jnp.einsum(
            "sij,sjhpk->sihpk", choose, pieces[1], preferred_element_type=jnp.float32
        ).astype(jnp.bfloat16)
        rim_held = jnp.einsum(
            "sij,sjkzc->sikzc", choose, pieces[2], preferred_element_type=jnp.float32
        ).astype(jnp.bfloat16)
        x_step = x_in[step]
        bc_part = jnp.einsum("sbd,dzk->sbzk", x_step, w_bc, preferred_element_type=jnp.float32)
        dt_part = jnp.einsum("sbd,dh->sbh", x_step, w_dt, preferred_element_type=jnp.float32)
        bc_sum, dt_sum = lax.psum((bc_part, dt_part), "beam")
        bc_new = stored(bc_sum)
        dt_raw = stored(dt_sum)
        bc_new = lax.dynamic_slice_in_dim(bc_new, beam_index * local_beams, local_beams, 1)
        dt_raw = lax.dynamic_slice_in_dim(dt_raw, beam_index * local_beams, local_beams, 1)
        inner_part = stored(
            lax.psum_scatter(
                jnp.einsum("sbd,dzhp->bszhp", x_step, w_inner4, preferred_element_type=jnp.float32),
                "beam",
                scatter_dimension=0,
                tiled=True,
            )
        )
        gate_in = jnp.transpose(inner_part[:, :, 0], (1, 0, 2, 3))
        x_new = jnp.transpose(inner_part[:, :, 1], (1, 0, 2, 3))
        mixed = jnp.sum(
            conv_held.astype(jnp.float32) * jnp.transpose(conv_taps[:-1], (1, 2, 0)), axis=-1
        )
        mixed = mixed + conv_taps[-1] * x_new.astype(jnp.float32)
        x_conv = stored(jax.nn.silu(mixed))
        conv_held = jnp.concatenate([conv_held[..., 1:], x_new[..., None]], axis=-1)
        mixed_bc = jnp.sum(rim_held.astype(jnp.float32) * bc_taps[:-1], axis=2) + bc_taps[
            -1
        ] * bc_new.astype(jnp.float32)
        bc_conv = stored(jax.nn.silu(mixed_bc))
        rim_held = jnp.concatenate([rim_held[:, :, 1:], bc_new[:, :, None]], axis=2)
        group_block = bc_conv
        for bit_number in range(swap_rounds):
            partner = partner_2(group_block, "row", bit_number)
            upper = jnp.bitwise_and(jnp.right_shift(row_index, bit_number), 1) == 1
            group_block = jnp.where(
                upper,
                jnp.concatenate([partner, group_block], axis=3),
                jnp.concatenate([group_block, partner], axis=3),
            )
        bc_group = group_block.astype(jnp.float32)
        b_in = bc_group[:, :, 0]
        c_out = bc_group[:, :, 1]
        step_size = jax.nn.softplus(dt_raw.astype(jnp.float32) + dt_bias)
        decay = jnp.exp(-decay_rates * step_size)
        x_val = x_conv.astype(jnp.float32)
        state = (
            decay[..., None, None] * ssm_held.astype(jnp.float32)
            + (step_size[..., None] * x_val)[..., None] * b_in[:, :, None, None, :]
        )
        read = jnp.sum(state * c_out[:, :, None, None, :], axis=-1) + d_skip[:, None] * x_val
        ssm_held = stored(state)
        gated = read * jax.nn.silu(gate_in.astype(jnp.float32))
        square_sum = jnp.sum(gated * gated, axis=(2, 3))
        stat_terms = square_sum[..., None] * group_mask
        totals = lax.psum(stat_terms, "row")
        mean_sq = lax.dynamic_index_in_dim(totals, group_index, 2, keepdims=False) / (
            group_heads * HDIM
        )
        normed = stored(gated * lax.rsqrt(mean_sq + EPS)[..., None, None] * gains)
        partial_out = jnp.einsum(
            "sbhp,hpd->sbd",
            lax.all_gather(normed, "beam", axis=1, tiled=True),
            w_out3,
            preferred_element_type=jnp.float32,
        )
        flat_rows = partial_out.reshape(sessions * width, partial_out.shape[2])
        outputs.append(
            lax.psum_scatter(flat_rows, "row", scatter_dimension=0, tiled=True).astype(jnp.bfloat16)
        )
    return (jnp.stack(outputs), ssm_held, conv_held, rim_held)


def solution(mesh):
    placed = (
        P(None, None, None, "beam"),
        P("beam", None, "row"),
        P("beam", None, "row"),
        P("beam", "row"),
        P(None, "row"),
        P(None, None, "row"),
        P("row"),
        P("row"),
        P("row"),
        P("row"),
        P("row", "beam"),
        P(None, "beam", "row", None, None),
        P(None, "beam", "row", None, None),
        P(None, "beam", None, None, "row"),
        P(),
    )
    return jax.shard_map(
        local,
        mesh=mesh,
        in_specs=placed,
        out_specs=(
            P(None, "row", "beam"),
            P(None, "beam", "row", None, None),
            P(None, "beam", "row", None, None),
            P(None, "beam", None, None, "row"),
        ),
        check_vma=False,
    )
```

profile of v0, /device:TPU:4, one launch (start us, length us, event | category | flops | bytes accessed | tf_op | source)
XLA Modules:
  0.0 760.4 jit_solution(5823953862466214772)
XLA Ops:
  7.2 4.8 copy.199
  12.1 1.1 convolution_bitcast_fusion.3
  14.0 1.1 convolution_bitcast_fusion.2
  16.0 1.1 convolution_bitcast_fusion.1
  17.0 0.8 copy.232
  17.9 1.1 convolution_bitcast_fusion
  19.9 2.3 copy.193
  24.1 22.1 %all-reduce.6 = (bf16[2,16,2,64]{3,1,2,0:T(8,128)(2,1)S(1)}, bf16[2,16,2,64]{3,1,2,0:T(8,128)(2,1)S(1)}, bf16[2,16,2,64]{3,1,2,0:T(8,128)(2,1)S(1)}, bf16[2,16,8...) all-reduce(f32[2,16,2,64]{3,1,2,0:T(8,128)S(1)} %fusion.30, ...), channel_id=1, replica_groups=mesh['beam'=8,'row'=32] {'beam'}, use_global_device_ids=true, to_apply=%region_22.23 | all-reduce | flops 17408 | bytes 104448 | tf_op jit(solution)/shard_map/psum | solution.py:82
  46.3 16.7 %all_gather.50 = bf16[2,16,3,2,64]{4,3,2,0,1:T(2,128)(2,1)S(1)} all-gather(bf16[2,2,3,2,64]{4,3,2,0,1:T(2,128)(2,1)S(1)} %copy.204), channel_id=1, replica_groups=mesh['beam'=8,'row'=32] {'beam'}, dimensions={1}, use_global_device_ids=true | all-gather | bytes 27648 | tf_op jit(solution)/shard_map/all_gather | solution.py:65
  63.3 12.8 %all_gather.54 = bf16[2,16,3,2,64]{4,3,2,0,1:T(2,128)(2,1)S(1)} all-gather(bf16[2,2,3,2,64]{4,3,2,0,1:T(2,128)(2,1)S(1)} %copy.220), channel_id=1, replica_groups=mesh['beam'=8,'row'=32] {'beam'}, dimensions={1}, use_global_device_ids=true | all-gather | bytes 27648 | tf_op jit(solution)/shard_map/all_gather | solution.py:65
  76.5 12.8 %all_gather.58 = bf16[2,16,3,2,64]{4,3,2,0,1:T(2,128)(2,1)S(1)} all-gather(bf16[2,2,3,2,64]{4,3,2,0,1:T(2,128)(2,1)S(1)} %copy.236), channel_id=1, replica_groups=mesh['beam'=8,'row'=32] {'beam'}, dimensions={1}, use_global_device_ids=true | all-gather | bytes 27648 | tf_op jit(solution)/shard_map/all_gather | solution.py:65
  89.6 12.8 %all_gather.62 = bf16[2,16,3,2,64]{4,3,2,0,1:T(2,128)(2,1)S(1)} all-gather(bf16[2,2,3,2,64]{4,3,2,0,1:T(2,128)(2,1)S(1)} %copy.252), channel_id=1, replica_groups=mesh['beam'=8,'row'=32] {'beam'}, dimensions={1}, use_global_device_ids=true | all-gather | bytes 27648 | tf_op jit(solution)/shard_map/all_gather | solution.py:65
  102.8 1.8 collective-permute-start
  104.6 12.8 %all_gather.49 = bf16[2,16,8,64,3]{3,2,4,0,1:T(8,128)(2,1)S(1)} all-gather(bf16[2,2,8,64,3]{3,2,4,0,1:T(8,128)(2,1)S(1)} %copy.196), channel_id=1, replica_groups=mesh['beam'=8,'row'=32] {'beam'}, dimensions={1}, use_global_device_ids=true | all-gather | bytes 110592 | tf_op jit(solution)/shard_map/all_gather | solution.py:64
  117.8 3.3 collective-permute-start.1
  121.4 1.3 collective-permute-done.1
  124.4 12.8 %all_gather.53 = bf16[2,16,8,64,3]{3,2,4,0,1:T(8,128)(2,1)S(1)} all-gather(bf16[2,2,8,64,3]{3,2,4,0,1:T(8,128)(2,1)S(1)} %copy.214), channel_id=1, replica_groups=mesh['beam'=8,'row'=32] {'beam'}, dimensions={1}, use_global_device_ids=true | all-gather | bytes 110592 | tf_op jit(solution)/shard_map/all_gather | solution.py:64
  138.4 12.8 %all_gather.57 = bf16[2,16,8,64,3]{3,2,4,0,1:T(8,128)(2,1)S(1)} all-gather(bf16[2,2,8,64,3]{3,2,4,0,1:T(8,128)(2,1)S(1)} %copy.230), channel_id=1, replica_groups=mesh['beam'=8,'row'=32] {'beam'}, dimensions={1}, use_global_device_ids=true | all-gather | bytes 110592 | tf_op jit(solution)/shard_map/all_gather | solution.py:64
  152.2 14.6 %all_gather.61 = bf16[2,16,8,64,3]{3,2,4,0,1:T(8,128)(2,1)S(1)} all-gather(bf16[2,2,8,64,3]{3,2,4,0,1:T(8,128)(2,1)S(1)} %copy.246), channel_id=1, replica_groups=mesh['beam'=8,'row'=32] {'beam'}, dimensions={1}, use_global_device_ids=true | all-gather | bytes 110592 | tf_op jit(solution)/shard_map/all_gather | solution.py:64
  167.4 39.3 %all-gather.5.cloned.1.call-done = bf16[2,16,8,64,256]{4,3,2,0,1:T(8,128)(2,1)} async-done(((bf16[2,2,8,64,256]{4,3,2,0,1:T(8,128)(2,1)}), bf16[2,16,8,64,256]{4,3,2,0,1:T(8,128)(2,1)}) %all-gather.5.cloned.1.call-update) | async-done | bytes 8388624 | tf_op jit(solution)/shard_map/all_gather | solution.py:63
  206.7 10.6 %multiply_reduce_fusion.3 = (f32[2,2,8,64]{1,3,2,0:T(8,128)S(1)}, bf16[2,2,8,64,256]{4,1,3,2,0:T(2,128)(2,1)S(1)}) fusion(f32[2,2,256]{2,1,0:T(2,128)S(1)} %get-tuple-element.64, f32[2,2,256]{2,1,0:T(2,128)S(1)} %get-tuple-element.65, f32[2,2,8,64]{1,3,2,0:T(8,128)S(1)} %copy.203, bf16[2,16,8,64,256]{4,3,2,0,1:T(8,128)(2,1)} %all-gather.5.cloned.1.call-done, ...), kind=kOutput, calls=%fused_computation.14 | convolution fusion | flops 20969536 | bytes 9461904 | tf_op jit(solution)/shard_map/sij,sjhpn->sihpn/dot_general | solution.py:70
  217.4 1.2 copy.210
  218.6 1.6 collective-permute-start.2
  220.3 2.0 collective-permute-done.2
  222.4 2.6 collective-permute-start.3
  225.0 1.9 collective-permute-done.3
  227.2 44.0 %all-gather.7.cloned.1.call-done = bf16[2,16,8,64,256]{4,3,2,0,1:T(8,128)(2,1)} async-done(((bf16[2,2,8,64,256]{4,3,2,0,1:T(8,128)(2,1)}), bf16[2,16,8,64,256]{4,3,2,0,1:T(8,128)(2,1)}) %all-gather.7.cloned.1.call-update) | async-done | bytes 8388624 | tf_op jit(solution)/shard_map/all_gather | solution.py:63
  271.2 10.6 %multiply_reduce_fusion.2 = (f32[2,2,8,64]{1,3,2,0:T(8,128)S(1)}, bf16[2,2,8,64,256]{4,1,3,2,0:T(2,128)(2,1)S(1)}) fusion(f32[2,2,256]{2,1,0:T(2,128)S(1)} %get-tuple-element.66, f32[2,2,256]{2,1,0:T(2,128)S(1)} %get-tuple-element.67, f32[2,2,8,64]{1,3,2,0:T(8,128)S(1)} %copy.219, bf16[2,16,8,64,256]{4,3,2,0,1:T(8,128)(2,1)} %all-gather.7.cloned.1.call-done, ...), kind=kOutput, calls=%fused_computation.12 | convolution fusion | flops 20969536 | bytes 9461904 | tf_op jit(solution)/shard_map/sij,sjhpn->sihpn/dot_general | solution.py:70
  281.8 1.2 copy.226
  283.1 1.8 collective-permute-start.4
  284.9 2.0 collective-permute-done.4
  287.0 2.6 collective-permute-start.5
  289.7 1.9 collective-permute-done.5
  291.8 43.8 %all-gather.9.cloned.1.call-done = bf16[2,16,8,64,256]{4,3,2,0,1:T(8,128)(2,1)} async-done(((bf16[2,2,8,64,256]{4,3,2,0,1:T(8,128)(2,1)}), bf16[2,16,8,64,256]{4,3,2,0,1:T(8,128)(2,1)}) %all-gather.9.cloned.1.call-update) | async-done | bytes 8388624 | tf_op jit(solution)/shard_map/all_gather | solution.py:63
  335.6 10.6 %multiply_reduce_fusion.1 = (f32[2,2,8,64]{1,3,2,0:T(8,128)S(1)}, bf16[2,2,8,64,256]{4,1,3,2,0:T(2,128)(2,1)S(1)}) fusion(f32[2,2,256]{2,1,0:T(2,128)S(1)} %get-tuple-element.68, f32[2,2,256]{2,1,0:T(2,128)S(1)} %get-tuple-element.69, f32[2,2,8,64]{1,3,2,0:T(8,128)S(1)} %copy.235, bf16[2,16,8,64,256]{4,3,2,0,1:T(8,128)(2,1)} %all-gather.9.cloned.1.call-done, ...), kind=kOutput, calls=%fused_computation.10 | convolution fusion | flops 20969536 | bytes 9461904 | tf_op jit(solution)/shard_map/sij,sjhpn->sihpn/dot_general | solution.py:70
  346.3 1.2 copy.242
  347.5 1.6 collective-permute-start.6
  349.2 2.0 collective-permute-done.6
  351.2 2.6 collective-permute-start.7
  357.5 42.7 %all-gather.11.cloned.1.call-done = bf16[2,16,8,64,256]{4,3,2,0,1:T(8,128)(2,1)} async-done(((bf16[2,2,8,64,256]{4,3,2,0,1:T(8,128)(2,1)}), bf16[2,16,8,64,256]{4,3,2,0,1:T(8,128)(2,1)}) %all-gather.11.cloned.1.call-update) | async-done | bytes 8388624 | tf_op jit(solution)/shard_map/all_gather | solution.py:63
  400.1 10.6 %fusion.172 = (bf16[2,2,8,64,256]{4,1,3,2,0:T(2,128)(2,1)S(1)}, f32[2,2,8,64]{1,3,2,0:T(8,128)S(1)}) fusion(f32[2,2,256]{2,1,0:T(2,128)S(1)} %get-tuple-element.70, f32[2,2,256]{2,1,0:T(2,128)S(1)} %get-tuple-element.71, f32[2,2,8,64]{1,3,2,0:T(8,128)S(1)} %copy.251, bf16[2,16,8,64,256]{4,3,2,0,1:T(8,128)(2,1)} %all-gather.11.cloned.1.call-done, ...), kind=kOutput, calls=%fused_computation.290 | convolution fusion | flops 20969536 | bytes 9461904 | tf_op jit(solution)/shard_map/sij,sjhpn->sihpn/dot_general | solution.py:70
  411.3 143.4 %all-reduce.5 = (f32[2,2,8]{1,0,2:T(2,128)S(1)}, f32[2,2,8]{1,0,2:T(2,128)S(1)}, f32[2,2,8]{1,0,2:T(2,128)S(1)}, f32[2,2,8]{1,0,2:T(2,128)S(1)}) all-reduce(f32[2,2,8]{1,0,2:T(2,128)S(1)} %get-tuple-element.105, f32[2,2,8]{1,0,2:T(2,128)S(1)} %get-tuple-element.104, ...), channel_id=1, replica_groups=mesh['beam'=8,'row'=32] {'row'}, use_global_device_ids=true, to_apply=%region_34.35 | all-reduce | flops 128 | bytes 1024 | tf_op jit(solution)/shard_map/psum | solution.py:132
  554.8 12.3 %all_gather.63 = bf16[2,16,8,64]{3,2,0,1:T(8,128)(2,1)S(1)} all-gather(bf16[2,2,8,64]{3,2,0,1:T(8,128)(2,1)S(1)} %copy.255), channel_id=1, replica_groups=mesh['beam'=8,'row'=32] {'beam'}, dimensions={1}, use_global_device_ids=true | all-gather | bytes 36864 | tf_op jit(solution)/shard_map/all_gather | solution.py:139
  567.4 12.7 %all_gather.59 = bf16[2,16,8,64]{3,2,0,1:T(8,128)(2,1)S(1)} all-gather(bf16[2,2,8,64]{3,2,0,1:T(8,128)(2,1)S(1)} %copy.239), channel_id=1, replica_groups=mesh['beam'=8,'row'=32] {'beam'}, dimensions={1}, use_global_device_ids=true | all-gather | bytes 36864 | tf_op jit(solution)/shard_map/all_gather | solution.py:139
  580.5 12.7 %all_gather.55 = bf16[2,16,8,64]{3,2,0,1:T(8,128)(2,1)S(1)} all-gather(bf16[2,2,8,64]{3,2,0,1:T(8,128)(2,1)S(1)} %copy.223), channel_id=1, replica_groups=mesh['beam'=8,'row'=32] {'beam'}, dimensions={1}, use_global_device_ids=true | all-gather | bytes 36864 | tf_op jit(solution)/shard_map/all_gather | solution.py:139
  593.6 12.7 %all_gather.51 = bf16[2,16,8,64]{3,2,0,1:T(8,128)(2,1)S(1)} all-gather(bf16[2,2,8,64]{3,2,0,1:T(8,128)(2,1)S(1)} %copy.207), channel_id=1, replica_groups=mesh['beam'=8,'row'=32] {'beam'}, dimensions={1}, use_global_device_ids=true | all-gather | bytes 36864 | tf_op jit(solution)/shard_map/all_gather | solution.py:139
  606.7 142.2 %all-reduce.8 = (bf16[32,1024]{1,0:T(8,128)(2,1)S(1)}, bf16[32,1024]{1,0:T(8,128)(2,1)S(1)}, bf16[32,1024]{1,0:T(8,128)(2,1)S(1)}, bf16[32,1024]{1,0:T(8,128)(2,1)S(1)}) all-reduce(f32[32,1024]{1,0:T(8,128)S(1)} %convolution_bitcast_fusion.4, ...), channel_id=9, replica_groups=mesh['beam'=8,'row'=32] {'row'}, use_global_device_ids=true, to_apply=%region_35.36.clone | all-reduce | flops 131072 | bytes 786432
  751.6 1.2 copy.259
  (182 shorter events, 20.9 us)
Async XLA Ops:
  7.2 559.9 %copy-start = (bf16[512,1024]{1,0:T(8,128)(2,1)S(1)}, bf16[512,1024]{1,0:T(8,128)(2,1)}, u32[]{:S(2)}) copy-start(bf16[512,1024]{1,0:T(8,128)(2,1)} %param.25) | copy-start | bytes 3145732
  7.2 4.9 copy-start.2
  7.2 115.6 %reduce-scatter.5.cloned.1.call-start = ((), (), s32[]{:S(2)}) async-start(), calls=%async_computation.5 | async-start | bytes 294912 | tf_op jit(solution)/shard_map/reduce_scatter | solution.py:88
  14.0 109.6 %reduce-scatter.7.cloned.1.call-start = ((), (), s32[]{:S(2)}) async-start(), calls=%async_computation.7 | async-start | bytes 294912 | tf_op jit(solution)/shard_map/reduce_scatter | solution.py:88
  15.9 121.6 %reduce-scatter.9.cloned.1.call-start = ((), (), s32[]{:S(2)}) async-start(), calls=%async_computation.9 | async-start | bytes 294912 | tf_op jit(solution)/shard_map/reduce_scatter | solution.py:88
  17.9 133.6 %reduce-scatter.11.cloned.1.call-start = ((), (), s32[]{:S(2)}) async-start(), calls=%async_computation.11 | async-start | bytes 294912 | tf_op jit(solution)/shard_map/reduce_scatter | solution.py:88
  19.0 3.3 copy-start.5
  19.0 3.4 copy-start.11
  19.0 4.1 copy-start.1
  19.9 26.4 %copy-start.6 = (bf16[2,2,3,2,64]{4,3,2,1,0:T(2,128)(2,1)S(1)}, bf16[2,2,3,2,64]{4,3,2,1,0:T(2,128)(2,1)}, u32[]{:S(2)}) copy-start(bf16[2,2,3,2,64]{4,3,2,1,0:T(2,128)(2,1)} %param.28) | copy-start | bytes 9220
  19.9 186.9 %all-gather.5.cloned.1.call-start = ((), (), s32[]{:S(2)}) async-start(), calls=%async_computation.4 | async-start | bytes 9437184 | tf_op jit(solution)/shard_map/all_gather | solution.py:63
  22.2 40.7 %copy-start.7 = (s32[4,2,16]{2,1,0:T(2,128)S(1)}, s32[4,2,16]{2,1,0:T(2,128)}, u32[]{:S(2)}) copy-start(s32[4,2,16]{2,1,0:T(2,128)} %param.29) | copy-start | bytes 1540
  22.2 82.3 %copy-start.4 = (bf16[2,2,8,64,3]{3,2,4,1,0:T(8,128)(2,1)S(1)}, bf16[2,2,8,64,3]{3,2,4,1,0:T(8,128)(2,1)}, u32[]{:S(2)}) copy-start(bf16[2,2,8,64,3]{3,2,4,1,0:T(8,128)(2,1)} %param.27) | copy-start | bytes 36868
  22.2 95.1 %copy-start.12 = (f32[8]{0:T(128)S(1)}, f32[8]{0:T(128)}, u32[]{:S(2)}) copy-start(f32[8]{0:T(128)} %param.22) | copy-start | bytes 100
  22.2 95.3 %copy-start.9 = (f32[8]{0:T(128)S(1)}, f32[8]{0:T(128)}, u32[]{:S(2)}) copy-start(f32[8]{0:T(128)} %param.21) | copy-start | bytes 100
  22.2 95.5 %copy-start.3 = (bf16[4,512]{1,0:T(4,128)(2,1)S(1)}, bf16[4,512]{1,0:T(4,128)(2,1)}, u32[]{:S(2)}) copy-start(bf16[4,512]{1,0:T(4,128)(2,1)} %param.19) | copy-start | bytes 12292
  22.3 248.9 %all-gather.7.cloned.1.call-start = ((), (), s32[]{:S(2)}) async-start(), calls=%async_computation.6 | async-start | bytes 9437184 | tf_op jit(solution)/shard_map/all_gather | solution.py:63
  102.8 15.0 %collective-permute-start = (bf16[2,2,2,64]{3,1,2,0:T(2,128)(2,1)S(1)}, bf16[2,2,2,64]{3,1,2,0:T(2,128)(2,1)S(1)}, u32[]{:S(2)}, u32[]{:S(2)}) collective-permute-start(bf16[2,2,2,64]{3,1,2,0:T(2,128)(2,1)S(1)} %get-tuple-element.101), channel_id=1, source_target_pairs={{0,1},{1,0},{2,3},{3,2},{4,5},{5,4},{6,7},{7,6},{8,9},{9,8},{10,11... | collective-permute-start | bytes 3080 | tf_op jit(solution)/shard_map/ppermute | solution.py:13
  117.8 4.9 collective-permute-start.1
  218.6 117.1 %all-gather.9.cloned.1.call-start = ((), (), s32[]{:S(2)}) async-start(), calls=%async_computation.8 | async-start | bytes 9437184 | tf_op jit(solution)/shard_map/all_gather | solution.py:63
  218.6 3.7 collective-permute-start.2
  222.4 4.5 collective-permute-start.3
  283.0 117.1 %all-gather.11.cloned.1.call-start = ((), (), s32[]{:S(2)}) async-start(), calls=%async_computation.10 | async-start | bytes 9437184 | tf_op jit(solution)/shard_map/all_gather | solution.py:63
  283.1 3.8 collective-permute-start.4
  287.0 4.5 collective-permute-start.5
  346.3 7.6 %copy-start.8 = (f32[512]{0:T(512)S(1)}, f32[512]{0:T(512)}, u32[]{:S(2)}) copy-start(f32[512]{0:T(512)} %param.24) | copy-start | bytes 6148
  346.3 8.3 %copy-start.13 = (u32[256]{0:T(256)S(1)}, u32[256]{0:T(256)}, u32[]{:S(2)}) copy-start(u32[256]{0:T(256)} %constant.86) | copy-start | bytes 3076
  347.5 3.7 collective-permute-start.6
  351.2 4.5 collective-permute-start.7
  400.1 10.8 %copy-start.10 = (f32[8]{0:T(128)S(1)}, f32[8]{0:T(128)}, u32[]{:S(2)}) copy-start(f32[8]{0:T(128)} %param.23) | copy-start | bytes 100
Sparse Core Ops, SparseCore 0:
  14.1 30.9 reduce-scatter.4
  47.8 31.9 reduce-scatter.6
  82.3 31.9 reduce-scatter.8
  116.8 32.1 reduce-scatter.10
  151.3 55.4 all-gather.4
  218.7 52.4 all-gather.6
  283.1 52.4 all-gather.8
  347.6 52.4 all-gather.10
where the time goes:
time: 769 us; the launch traced here: 760 us
  blocking collectives  466 us (61%)
  waiting for transfers between devices  182 us (24%)
  matrix products  51.5 us (7%)
  local copies, waits for them, and re-layouts  25.6 us (3%)
  starting transfers between devices  18.3 us (2%)
  between operations  15 us (2%)
    all_gather x4, waiting for transfers between devices, local(): lax.all_gather(ssm_held, 'beam', axis=1, tiled=True)  170 us
    psum x1, blocking collectives, local(): totals = lax.psum(stat_terms, 'row')  143 us
    unnamed x1, blocking collectives  142 us
    all_gather x4, blocking collectives, local(): lax.all_gather(rim_held, 'beam', axis=1, tiled=True)  55.1 us
    all_gather x4, blocking collectives, local(): lax.all_gather(conv_held, 'beam', axis=1, tiled=True)  52.9 us
    all_gather x4, blocking collectives, local(): lax.all_gather(normed, 'beam', axis=1, tiled=True)  50.6 us
    dot_general x4, matrix products, local(): jnp.einsum('sij,sjhpn->sihpn', choose, pieces[0], preferred_element_type=...  42.5 us
    psum x1, blocking collectives, local(): bc_sum, dt_sum = lax.psum((bc_part, dt_part), 'beam')  22.1 us
  transfers between devices with their start and end apart: 16, of which 11 were waited for; matrix products, arithmetic and copies ran while one was open for 3% of the time, Pallas kernels for 0%

commit v1 on v0

--- a/solution.py
+++ b/solution.py
@@ -1,3 +1,4 @@
+import functools
 import jax
 import jax.numpy as jnp
 from jax import lax
@@ -7,6 +8,19 @@
 HDIM = 64
 GROUPS = 8
 EPS = 1e-05
+
+
+def enter_roots_by_axis(arr_in, named_axis):
+    a_now = lax.all_to_all(
+        jnp.stack([arr_in for _ in range(lax.axis_size(named_axis))], 0),
+        concat_axis=0,
+        split_axis=0,
+        axis_name=named_axis,
+    )
+    return jnp.concatenate(a_now, 1)
+
+
+rings_tell = functools.partial(enter_roots_by_axis, named_axis="beam")
 
 
 def partner_2(shard, axis, stride):
@@ -135,10 +149,7 @@
         )
         normed = stored(gated * lax.rsqrt(mean_sq + EPS)[..., None, None] * gains)
         partial_out = jnp.einsum(
-            "sbhp,hpd->sbd",
-            lax.all_gather(normed, "beam", axis=1, tiled=True),
-            w_out3,
-            preferred_element_type=jnp.float32,
+            "sbhp,hpd->sbd", rings_tell(normed), w_out3, preferred_element_type=jnp.float32
         )
         flat_rows = partial_out.reshape(sessions * width, partial_out.shape[2])
         outputs.append(

time: 769 us -> 752 us (0.978)
  blocking collectives: 466 us -> 416 us
  starting transfers between devices: 18.3 us -> 39.8 us
    all_gather x4 -> x0, blocking collectives: 50.6 us -> none  [local(): lax.all_gather(normed, 'beam', axis=1, tiled=True)]
    all_to_all x0 -> x4, starting transfers between devices: none -> 21.5 us  [enter_roots_by_axis(): lax.all_to_all(jnp.stack([arr_in for _ in range(lax.axis_size(named_axis)...]
  transfers between devices with their start and end apart: 16 -> 20, of which waited for: 11 -> 14; matrix products, arithmetic and copies ran while one was open for 3% -> 3% of each run, Pallas kernels for 0% -> 0%
where the time goes in v1:
time: 752 us; the launch traced here: 743 us
  blocking collectives  416 us (55%)
  waiting for transfers between devices  189 us (25%)
  matrix products  51.5 us (7%)
  starting transfers between devices  39.8 us (5%)
  local copies, waits for them, and re-layouts  29.5 us (4%)
  between operations  15.2 us (2%)
    all_gather x4, waiting for transfers between devices, local(): lax.all_gather(ssm_held, 'beam', axis=1, tiled=True)  170 us
    psum x1, blocking collectives, local(): totals = lax.psum(stat_terms, 'row')  143 us
    unnamed x1, blocking collectives  142 us
    all_gather x4, blocking collectives, local(): lax.all_gather(rim_held, 'beam', axis=1, tiled=True)  55.1 us
    all_gather x4, blocking collectives, local(): lax.all_gather(conv_held, 'beam', axis=1, tiled=True)  52.9 us
    dot_general x4, matrix products, local(): jnp.einsum('sij,sjhpn->sihpn', choose, pieces[0], preferred_element_type=...  42.5 us
    psum x1, blocking collectives, local(): bc_sum, dt_sum = lax.psum((bc_part, dt_part), 'beam')  22.1 us
    all_to_all x4, starting transfers between devices, enter_roots_by_axis(): lax.all_to_all(jnp.stack([arr_in for _ in range(lax.axis_size(named_axis)...  21.5 us
  transfers between devices with their start and end apart: 20, of which 14 were waited for; matrix products, arithmetic and copies ran while one was open for 3% of the time, Pallas kernels for 0%

profile of v1, /device:TPU:4, one launch (start us, length us, event | category | flops | bytes accessed | tf_op | source)
XLA Modules:
  0.0 742.6 jit_solution(16865093424822446280)
XLA Ops:
  7.2 4.8 copy.191
  12.1 1.1 convolution_bitcast_fusion.3
  16.0 1.1 convolution_bitcast_fusion.1
  19.9 2.3 copy.185
  24.1 22.1 %all-reduce.6 = (bf16[2,16,2,64]{3,1,2,0:T(8,128)(2,1)S(1)}, bf16[2,16,2,64]{3,1,2,0:T(8,128)(2,1)S(1)}, bf16[2,16,2,64]{3,1,2,0:T(8,128)(2,1)S(1)}, bf16[2,16,8...) all-reduce(f32[2,16,2,64]{3,1,2,0:T(8,128)S(1)} %fusion.30, ...), channel_id=1, replica_groups=mesh['beam'=8,'row'=32] {'beam'}, use_global_device_ids=true, to_apply=%region_22.23 | all-reduce | flops 17408 | bytes 104448 | tf_op jit(solution)/shard_map/psum | solution.py:96
  46.3 16.7 %all_gather.38 = bf16[2,16,3,2,64]{4,3,2,0,1:T(2,128)(2,1)S(1)} all-gather(bf16[2,2,3,2,64]{4,3,2,0,1:T(2,128)(2,1)S(1)} %copy.196), channel_id=1, replica_groups=mesh['beam'=8,'row'=32] {'beam'}, dimensions={1}, use_global_device_ids=true | all-gather | bytes 27648 | tf_op jit(solution)/shard_map/all_gather | solution.py:79
  63.3 12.8 %all_gather.41 = bf16[2,16,3,2,64]{4,3,2,0,1:T(2,128)(2,1)S(1)} all-gather(bf16[2,2,3,2,64]{4,3,2,0,1:T(2,128)(2,1)S(1)} %copy.211), channel_id=1, replica_groups=mesh['beam'=8,'row'=32] {'beam'}, dimensions={1}, use_global_device_ids=true | all-gather | bytes 27648 | tf_op jit(solution)/shard_map/all_gather | solution.py:79
  76.5 12.8 %all_gather.44 = bf16[2,16,3,2,64]{4,3,2,0,1:T(2,128)(2,1)S(1)} all-gather(bf16[2,2,3,2,64]{4,3,2,0,1:T(2,128)(2,1)S(1)} %copy.226), channel_id=1, replica_groups=mesh['beam'=8,'row'=32] {'beam'}, dimensions={1}, use_global_device_ids=true | all-gather | bytes 27648 | tf_op jit(solution)/shard_map/all_gather | solution.py:79
  89.6 12.8 %all_gather.47 = bf16[2,16,3,2,64]{4,3,2,0,1:T(2,128)(2,1)S(1)} all-gather(bf16[2,2,3,2,64]{4,3,2,0,1:T(2,128)(2,1)S(1)} %copy.241), channel_id=1, replica_groups=mesh['beam'=8,'row'=32] {'beam'}, dimensions={1}, use_global_device_ids=true | all-gather | bytes 27648 | tf_op jit(solution)/shard_map/all_gather | solution.py:79
  102.8 1.8 collective-permute-start
  104.6 12.8 %all_gather.37 = bf16[2,16,8,64,3]{3,2,4,0,1:T(8,128)(2,1)S(1)} all-gather(bf16[2,2,8,64,3]{3,2,4,0,1:T(8,128)(2,1)S(1)} %copy.188), channel_id=1, replica_groups=mesh['beam'=8,'row'=32] {'beam'}, dimensions={1}, use_global_device_ids=true | all-gather | bytes 110592 | tf_op jit(solution)/shard_map/all_gather | solution.py:78
  117.8 3.3 collective-permute-start.1
  121.5 1.3 collective-permute-done.1
  124.4 12.8 %all_gather.40 = bf16[2,16,8,64,3]{3,2,4,0,1:T(8,128)(2,1)S(1)} all-gather(bf16[2,2,8,64,3]{3,2,4,0,1:T(8,128)(2,1)S(1)} %copy.205), channel_id=1, replica_groups=mesh['beam'=8,'row'=32] {'beam'}, dimensions={1}, use_global_device_ids=true | all-gather | bytes 110592 | tf_op jit(solution)/shard_map/all_gather | solution.py:78
  138.4 12.8 %all_gather.43 = bf16[2,16,8,64,3]{3,2,4,0,1:T(8,128)(2,1)S(1)} all-gather(bf16[2,2,8,64,3]{3,2,4,0,1:T(8,128)(2,1)S(1)} %copy.220), channel_id=1, replica_groups=mesh['beam'=8,'row'=32] {'beam'}, dimensions={1}, use_global_device_ids=true | all-gather | bytes 110592 | tf_op jit(solution)/shard_map/all_gather | solution.py:78
  152.3 14.5 %all_gather.46 = bf16[2,16,8,64,3]{3,2,4,0,1:T(8,128)(2,1)S(1)} all-gather(bf16[2,2,8,64,3]{3,2,4,0,1:T(8,128)(2,1)S(1)} %copy.235), channel_id=1, replica_groups=mesh['beam'=8,'row'=32] {'beam'}, dimensions={1}, use_global_device_ids=true | all-gather | bytes 110592 | tf_op jit(solution)/shard_map/all_gather | solution.py:78
  167.4 39.3 %all-gather.5.cloned.1.call-done = bf16[2,16,8,64,256]{4,3,2,0,1:T(8,128)(2,1)} async-done(((bf16[2,2,8,64,256]{4,3,2,0,1:T(8,128)(2,1)}), bf16[2,16,8,64,256]{4,3,2,0,1:T(8,128)(2,1)}) %all-gather.5.cloned.1.call-update) | async-done | bytes 8388624 | tf_op jit(solution)/shard_map/all_gather | solution.py:77
  206.7 10.6 %multiply_reduce_fusion.3 = (f32[2,2,8,64]{1,3,2,0:T(8,128)S(1)}, bf16[2,2,8,64,256]{4,1,3,2,0:T(2,128)(2,1)S(1)}) fusion(f32[2,2,256]{2,1,0:T(2,128)S(1)} %get-tuple-element.64, f32[2,2,256]{2,1,0:T(2,128)S(1)} %get-tuple-element.65, f32[2,2,8,64]{1,3,2,0:T(8,128)S(1)} %copy.195, bf16[2,16,8,64,256]{4,3,2,0,1:T(8,128)(2,1)} %all-gather.5.cloned.1.call-done, ...), kind=kOutput, calls=%fused_computation.14 | convolution fusion | flops 20969536 | bytes 9461904 | tf_op jit(solution)/shard_map/sij,sjhpn->sihpn/dot_general | solution.py:84
  217.3 1.2 copy.201
  218.6 1.7 collective-permute-start.2
  220.3 2.0 collective-permute-done.2
  222.3 2.6 collective-permute-start.3
  225.0 1.9 collective-permute-done.3
  227.2 44.0 %all-gather.7.cloned.1.call-done = bf16[2,16,8,64,256]{4,3,2,0,1:T(8,128)(2,1)} async-done(((bf16[2,2,8,64,256]{4,3,2,0,1:T(8,128)(2,1)}), bf16[2,16,8,64,256]{4,3,2,0,1:T(8,128)(2,1)}) %all-gather.7.cloned.1.call-update) | async-done | bytes 8388624 | tf_op jit(solution)/shard_map/all_gather | solution.py:77
  271.1 10.6 %multiply_reduce_fusion.2 = (f32[2,2,8,64]{1,3,2,0:T(8,128)S(1)}, bf16[2,2,8,64,256]{4,1,3,2,0:T(2,128)(2,1)S(1)}) fusion(f32[2,2,256]{2,1,0:T(2,128)S(1)} %get-tuple-element.66, f32[2,2,256]{2,1,0:T(2,128)S(1)} %get-tuple-element.67, f32[2,2,8,64]{1,3,2,0:T(8,128)S(1)} %copy.210, bf16[2,16,8,64,256]{4,3,2,0,1:T(8,128)(2,1)} %all-gather.7.cloned.1.call-done, ...), kind=kOutput, calls=%fused_computation.12 | convolution fusion | flops 20969536 | bytes 9461904 | tf_op jit(solution)/shard_map/sij,sjhpn->sihpn/dot_general | solution.py:84
  281.8 1.2 copy.216
  283.0 1.8 collective-permute-start.4
  284.8 2.0 collective-permute-done.4
  287.0 2.6 collective-permute-start.5
  289.6 1.9 collective-permute-done.5
  291.8 43.8 %all-gather.9.cloned.1.call-done = bf16[2,16,8,64,256]{4,3,2,0,1:T(8,128)(2,1)} async-done(((bf16[2,2,8,64,256]{4,3,2,0,1:T(8,128)(2,1)}), bf16[2,16,8,64,256]{4,3,2,0,1:T(8,128)(2,1)}) %all-gather.9.cloned.1.call-update) | async-done | bytes 8388624 | tf_op jit(solution)/shard_map/all_gather | solution.py:77
  335.6 10.6 %multiply_reduce_fusion.1 = (f32[2,2,8,64]{1,3,2,0:T(8,128)S(1)}, bf16[2,2,8,64,256]{4,1,3,2,0:T(2,128)(2,1)S(1)}) fusion(f32[2,2,256]{2,1,0:T(2,128)S(1)} %get-tuple-element.68, f32[2,2,256]{2,1,0:T(2,128)S(1)} %get-tuple-element.69, f32[2,2,8,64]{1,3,2,0:T(8,128)S(1)} %copy.225, bf16[2,16,8,64,256]{4,3,2,0,1:T(8,128)(2,1)} %all-gather.9.cloned.1.call-done, ...), kind=kOutput, calls=%fused_computation.10 | convolution fusion | flops 20969536 | bytes 9461904 | tf_op jit(solution)/shard_map/sij,sjhpn->sihpn/dot_general | solution.py:84
  346.3 1.2 copy.231
  347.5 1.6 collective-permute-start.6
  349.1 2.0 collective-permute-done.6
  351.2 2.6 collective-permute-start.7
  357.4 42.7 %all-gather.11.cloned.1.call-done = bf16[2,16,8,64,256]{4,3,2,0,1:T(8,128)(2,1)} async-done(((bf16[2,2,8,64,256]{4,3,2,0,1:T(8,128)(2,1)}), bf16[2,16,8,64,256]{4,3,2,0,1:T(8,128)(2,1)}) %all-gather.11.cloned.1.call-update) | async-done | bytes 8388624 | tf_op jit(solution)/shard_map/all_gather | solution.py:77
  400.1 10.6 %fusion.168 = (bf16[2,2,8,64,256]{4,1,3,2,0:T(2,128)(2,1)S(1)}, f32[2,2,8,64]{1,3,2,0:T(8,128)S(1)}) fusion(f32[2,2,256]{2,1,0:T(2,128)S(1)} %get-tuple-element.70, f32[2,2,256]{2,1,0:T(2,128)S(1)} %get-tuple-element.71, f32[2,2,8,64]{1,3,2,0:T(8,128)S(1)} %copy.240, bf16[2,16,8,64,256]{4,3,2,0,1:T(8,128)(2,1)} %all-gather.11.cloned.1.call-done, ...), kind=kOutput, calls=%fused_computation.286 | convolution fusion | flops 20969536 | bytes 9461904 | tf_op jit(solution)/shard_map/sij,sjhpn->sihpn/dot_general | solution.py:84
  411.2 143.4 %all-reduce.5 = (f32[2,2,8]{1,0,2:T(2,128)S(1)}, f32[2,2,8]{1,0,2:T(2,128)S(1)}, f32[2,2,8]{1,0,2:T(2,128)S(1)}, f32[2,2,8]{1,0,2:T(2,128)S(1)}) all-reduce(f32[2,2,8]{1,0,2:T(2,128)S(1)} %get-tuple-element.105, f32[2,2,8]{1,0,2:T(2,128)S(1)} %get-tuple-element.104, ...), channel_id=1, replica_groups=mesh['beam'=8,'row'=32] {'row'}, use_global_device_ids=true, to_apply=%region_34.35 | all-reduce | flops 128 | bytes 1024 | tf_op jit(solution)/shard_map/psum | solution.py:146
  555.5 4.9 all-to-all-start.3
  562.7 1.2 copy.247
  563.9 5.2 all-to-all-start.2
  569.3 2.8 all-to-all-done.2
  572.1 5.7 all-to-all-start.1
  578.7 2.1 all-to-all-done.1
  580.8 5.7 all-to-all-start
  587.1 2.5 all-to-all-done
  590.1 142.2 %all-reduce.8 = (bf16[32,1024]{1,0:T(8,128)(2,1)S(1)}, bf16[32,1024]{1,0:T(8,128)(2,1)S(1)}, bf16[32,1024]{1,0:T(8,128)(2,1)S(1)}, bf16[32,1024]{1,0:T(8,128)(2,1)S(1)}) all-reduce(f32[32,1024]{1,0:T(8,128)S(1)} %convolution_bitcast_fusion.4, ...), channel_id=9, replica_groups=mesh['beam'=8,'row'=32] {'row'}, use_global_device_ids=true, to_apply=%region_35.36.clone | all-reduce | flops 131072 | bytes 786432
  (202 shorter events, 27.8 us)
Async XLA Ops:
  7.2 570.9 %copy-start = (bf16[512,1024]{1,0:T(8,128)(2,1)S(1)}, bf16[512,1024]{1,0:T(8,128)(2,1)}, u32[]{:S(2)}) copy-start(bf16[512,1024]{1,0:T(8,128)(2,1)} %param.25) | copy-start | bytes 3145732
  7.2 4.9 copy-start.2
  7.2 115.6 %reduce-scatter.5.cloned.1.call-start = ((), (), s32[]{:S(2)}) async-start(), calls=%async_computation.9 | async-start | bytes 294912 | tf_op jit(solution)/shard_map/reduce_scatter | solution.py:102
  14.0 109.6 %reduce-scatter.7.cloned.1.call-start = ((), (), s32[]{:S(2)}) async-start(), calls=%async_computation.11 | async-start | bytes 294912 | tf_op jit(solution)/shard_map/reduce_scatter | solution.py:102
  15.9 121.6 %reduce-scatter.9.cloned.1.call-start = ((), (), s32[]{:S(2)}) async-start(), calls=%async_computation.13 | async-start | bytes 294912 | tf_op jit(solution)/shard_map/reduce_scatter | solution.py:102
  17.9 133.6 %reduce-scatter.11.cloned.1.call-start = ((), (), s32[]{:S(2)}) async-start(), calls=%async_computation.15 | async-start | bytes 294912 | tf_op jit(solution)/shard_map/reduce_scatter | solution.py:102
  19.0 3.3 copy-start.5
  19.0 3.3 copy-start.11
  19.0 4.1 copy-start.1
  19.9 26.4 %copy-start.6 = (bf16[2,2,3,2,64]{4,3,2,1,0:T(2,128)(2,1)S(1)}, bf16[2,2,3,2,64]{4,3,2,1,0:T(2,128)(2,1)}, u32[]{:S(2)}) copy-start(bf16[2,2,3,2,64]{4,3,2,1,0:T(2,128)(2,1)} %param.28) | copy-start | bytes 9220
  19.9 186.8 %all-gather.5.cloned.1.call-start = ((), (), s32[]{:S(2)}) async-start(), calls=%async_computation.8 | async-start | bytes 9437184 | tf_op jit(solution)/shard_map/all_gather | solution.py:77
  22.2 40.7 %copy-start.7 = (s32[4,2,16]{2,1,0:T(2,128)S(1)}, s32[4,2,16]{2,1,0:T(2,128)}, u32[]{:S(2)}) copy-start(s32[4,2,16]{2,1,0:T(2,128)} %param.29) | copy-start | bytes 1540
  22.2 82.3 %copy-start.4 = (bf16[2,2,8,64,3]{3,2,4,1,0:T(8,128)(2,1)S(1)}, bf16[2,2,8,64,3]{3,2,4,1,0:T(8,128)(2,1)}, u32[]{:S(2)}) copy-start(bf16[2,2,8,64,3]{3,2,4,1,0:T(8,128)(2,1)} %param.27) | copy-start | bytes 36868
  22.2 95.1 %copy-start.12 = (f32[8]{0:T(128)S(1)}, f32[8]{0:T(128)}, u32[]{:S(2)}) copy-start(f32[8]{0:T(128)} %param.22) | copy-start | bytes 100
  22.2 95.3 %copy-start.9 = (f32[8]{0:T(128)S(1)}, f32[8]{0:T(128)}, u32[]{:S(2)}) copy-start(f32[8]{0:T(128)} %param.21) | copy-start | bytes 100
  22.3 95.5 %copy-start.3 = (bf16[4,512]{1,0:T(4,128)(2,1)S(1)}, bf16[4,512]{1,0:T(4,128)(2,1)}, u32[]{:S(2)}) copy-start(bf16[4,512]{1,0:T(4,128)(2,1)} %param.19) | copy-start | bytes 12292
  22.3 248.9 %all-gather.7.cloned.1.call-start = ((), (), s32[]{:S(2)}) async-start(), calls=%async_computation.10 | async-start | bytes 9437184 | tf_op jit(solution)/shard_map/all_gather | solution.py:77
  102.8 15.0 %collective-permute-start = (bf16[2,2,2,64]{3,1,2,0:T(2,128)(2,1)S(1)}, bf16[2,2,2,64]{3,1,2,0:T(2,128)(2,1)S(1)}, u32[]{:S(2)}, u32[]{:S(2)}) collective-permute-start(bf16[2,2,2,64]{3,1,2,0:T(2,128)(2,1)S(1)} %get-tuple-element.101), channel_id=1, source_target_pairs={{0,1},{1,0},{2,3},{3,2},{4,5},{5,4},{6,7},{7,6},{8,9},{9,8},{10,11... | collective-permute-start | bytes 3080 | tf_op jit(solution)/shard_map/ppermute | solution.py:27
  117.8 4.9 collective-permute-start.1
  218.5 117.1 %all-gather.9.cloned.1.call-start = ((), (), s32[]{:S(2)}) async-start(), calls=%async_computation.12 | async-start | bytes 9437184 | tf_op jit(solution)/shard_map/all_gather | solution.py:77
  218.6 3.7 collective-permute-start.2
  222.3 4.5 collective-permute-start.3
  283.0 117.1 %all-gather.11.cloned.1.call-start = ((), (), s32[]{:S(2)}) async-start(), calls=%async_computation.14 | async-start | bytes 9437184 | tf_op jit(solution)/shard_map/all_gather | solution.py:77
  283.0 3.8 collective-permute-start.4
  287.0 4.5 collective-permute-start.5
  346.2 7.6 %copy-start.8 = (f32[512]{0:T(512)S(1)}, f32[512]{0:T(512)}, u32[]{:S(2)}) copy-start(f32[512]{0:T(512)} %param.24) | copy-start | bytes 6148
  346.2 8.3 %copy-start.13 = (u32[256]{0:T(256)S(1)}, u32[256]{0:T(256)}, u32[]{:S(2)}) copy-start(u32[256]{0:T(256)} %constant.86) | copy-start | bytes 3076
  347.5 3.7 collective-permute-start.6
  351.2 4.5 collective-permute-start.7
  400.1 10.8 %copy-start.10 = (f32[8]{0:T(128)S(1)}, f32[8]{0:T(128)}, u32[]{:S(2)}) copy-start(f32[8]{0:T(128)} %param.23) | copy-start | bytes 100
  555.5 8.4 %all-to-all-start.3 = ((bf16[8,2,1024]{2,1,0:T(2,128)(2,1)}), bf16[8,2,1024]{2,1,0:T(2,128)(2,1)S(1)}, u32[]{:S(2)}, u32[]{:S(2)}) async-start(bf16[8,2,1024]{2,1,0:T(2,128)(2,1)} %reshape.199), calls=%async_computation.7 | async-start | bytes 65536 | tf_op jit(solution)/shard_map/all_to_all | solution.py:14
  563.9 8.2 %all-to-all-start.2 = ((bf16[8,2,1024]{2,1,0:T(2,128)(2,1)}), bf16[8,2,1024]{2,1,0:T(2,128)(2,1)S(1)}, u32[]{:S(2)}, u32[]{:S(2)}) async-start(bf16[8,2,1024]{2,1,0:T(2,128)(2,1)} %reshape.201), calls=%async_computation.5 | async-start | bytes 65536 | tf_op jit(solution)/shard_map/all_to_all | solution.py:14
  572.1 8.7 %all-to-all-start.1 = ((bf16[8,2,1024]{2,1,0:T(2,128)(2,1)}), bf16[8,2,1024]{2,1,0:T(2,128)(2,1)S(1)}, u32[]{:S(2)}, u32[]{:S(2)}) async-start(bf16[8,2,1024]{2,1,0:T(2,128)(2,1)} %reshape.203), calls=%async_computation.3 | async-start | bytes 65536 | tf_op jit(solution)/shard_map/all_to_all | solution.py:14
  580.8 8.7 %all-to-all-start = ((bf16[8,2,1024]{2,1,0:T(2,128)(2,1)}), bf16[8,2,1024]{2,1,0:T(2,128)(2,1)S(1)}, u32[]{:S(2)}, u32[]{:S(2)}) async-start(bf16[8,2,1024]{2,1,0:T(2,128)(2,1)} %reshape.205), calls=%async_computation.1 | async-start | bytes 65536 | tf_op jit(solution)/shard_map/all_to_all | solution.py:14
Sparse Core Ops, SparseCore 0:
  14.1 30.9 reduce-scatter.4
  47.8 31.8 reduce-scatter.6
  82.2 31.9 reduce-scatter.8
  116.8 32.1 reduce-scatter.10
  151.3 55.3 all-gather.4
  218.7 52.4 all-gather.6
  283.1 52.4 all-gather.8
  347.6 52.4 all-gather.10
